TPU v7x, 32 devices: a whole 2x2x4 slice. The times are simulated.
32 devices in a mesh: groups: 2 (over y), row: 16 (over z, x, core).
Axes of the slice: x: 2, y: 2, z: 4, core: 2. Of those that a mesh axis runs over, the one named last changes fastest.
Arguments:
- activations: bfloat16 [768, 8192], P('groups', 'row'), parts along dimension 0, may hold values from -24 to 24
- norm_gain: bfloat16 [8192], P('row'), may hold values from 0.099609375 to 1.8984375
- gate_weight: bfloat16 [8192, 28672], P(None, 'row'), may hold values from -0.0625 to 0.0625
- up_weight: bfloat16 [8192, 28672], P(None, 'row'), may hold values from -0.0625 to 0.0625
- down_weight: bfloat16 [28672, 8192], P('row'), may hold values from -0.046875 to 0.046875
Outputs:
- mlp_out: bfloat16 [768, 8192], P('groups', 'row'), parts along dimension 0
There are 2 independent parts, one for each index of `groups`. A program takes and returns all parts, laid end to end along the dimension named above; an argument that names none is the same for every part. Nothing has to cross between parts.
All inputs are finite; a program needn't handle non-finite values.
Results may differ from a plain program's by a relative error of at most 0.0065.
Values may be sent and summed in bfloat16 or wider, within the bound.
A program may use at most 192 MiB of HBM per device.

v0:
```python
import jax
import jax.numpy as jnp
from jax import lax
from jax.sharding import PartitionSpec as P

D = 8192


def per_device(activations, norm_gain, gate_weight, up_weight, down_weight):
    float_rows = activations.astype(jnp.float32)
    square_sums = lax.psum(jnp.sum(float_rows * float_rows, axis=1), "row")
    inv_scale = lax.rsqrt(square_sums / D + 1e-05)
    normed = (float_rows * inv_scale[:, None] * norm_gain.astype(jnp.float32)[None, :]).astype(
        jnp.bfloat16
    )
    shard_rows = lax.all_gather(normed, "row", axis=1, tiled=True)
    gate_proj = jnp.dot(shard_rows, gate_weight, preferred_element_type=jnp.float32)
    up_proj = jnp.dot(shard_rows, up_weight, preferred_element_type=jnp.float32)
    hidden = (jax.nn.silu(gate_proj) * up_proj).astype(jnp.bfloat16)
    reduced = lax.psum_scatter(
        lax.dot_general(
            down_weight, hidden, (((0,), (1,)), ((), ())), preferred_element_type=jnp.float32
        ),
        "row",
        scatter_dimension=0,
        tiled=True,
    )
    return reduced.T.astype(jnp.bfloat16)


def solution(mesh):
    in_specs = (P("groups", "row"), P("row"), P(None, "row"), P(None, "row"), P("row", None))
    out_specs = P("groups", "row")
    return jax.shard_map(
        per_device, mesh=mesh, in_specs=in_specs, out_specs=out_specs, check_vma=False
    )
```

profile of v0, /device:TPU:0, one launch (start us, length us, event | category | flops | bytes accessed | tf_op | source)
XLA Modules:
  0.0 305.9 jit_solution(5603079134771323414)
XLA Ops:
  6.5 0.0 all-gather.2.cloned.1.call-start
  6.5 0.7 convert_element_type.19
  7.2 1.2 fusion.1
  8.4 34.9 %psum.7 = f32[384]{0:T(512)S(1)} all-reduce(f32[384]{0:T(512)S(1)} %fusion.1), channel_id=1, replica_groups=mesh['groups'=2,'row'=16] {'row'}, use_global_device_ids=true, to_apply=%region_1.0 | all-reduce | flops 384 | bytes 3072 | tf_op jit(solution)/shard_map/psum | solution.py:11
  43.3 1.9 fusion.3
  45.2 0.0 all-gather.2.cloned.1.call-update
  45.2 0.0 reduce-scatter.2.cloned.1.call-start
  45.3 62.6 %all-gather.2.cloned.1.call-done = bf16[384,8192]{1,0:T(8,128)(2,1)} async-done(((bf16[384,512]{1,0:T(8,128)(2,1)}), bf16[384,8192]{1,0:T(8,128)(2,1)}) %all-gather.2.cloned.1.call-update) | async-done | bytes 6291472 | tf_op jit(solution)/shard_map/all_gather | solution.py:16
  107.9 0.0 copy-start
  107.9 19.6 %fusion.4 = f32[384,1792]{1,0:T(8,128)} fusion(bf16[384,8192]{1,0:T(8,128)(2,1)} %all-gather.2.cloned.1.call-done, bf16[8192,1792]{1,0:T(8,128)(2,1)} %param.7), kind=kOutput, calls=%fused_computation.10 | convolution fusion | flops 11274289152 | bytes 38404096 | tf_op jit(solution)/shard_map/dot_general | solution.py:17
  127.5 0.0 copy-done
  127.5 16.7 %fusion = bf16[384,1792]{1,0:T(8,128)(2,1)S(1)} fusion(bf16[384,8192]{1,0:T(8,128)(2,1)S(1)} %copy-done, bf16[8192,1792]{1,0:T(8,128)(2,1)} %param.8, f32[384,1792]{1,0:T(8,128)} %fusion.4), kind=kOutput, calls=%fused_computation.2 | convolution fusion | flops 11278417920 | bytes 39780352 | tf_op jit(solution)/shard_map/dot_general | solution.py:18
  144.2 19.8 %convolution_bitcast_fusion = f32[8192,384]{0,1:T(8,128)} fusion(bf16[384,1792]{1,0:T(8,128)(2,1)S(1)} %fusion, bf16[1792,8192]{1,0:T(8,128)(2,1)} %param.9), kind=kOutput, calls=%fused_computation | convolution fusion | flops 11274289152 | bytes 43319296 | tf_op jit(solution)/shard_map/dot_general | solution.py:21
  164.0 0.0 reduce-scatter.2.cloned.1.call-update
  164.0 133.1 %reduce-scatter.2.cloned.1.call-done = f32[512,384]{0,1:T(8,128)} async-done(((f32[8192,384]{0,1:T(8,128)}), f32[512,384]{0,1:T(8,128)}) %reduce-scatter.2.cloned.1.call-update) | async-done | bytes 786448 | tf_op jit(solution)/shard_map/reduce_scatter | solution.py:20
  297.1 1.9 convert_bitcast_fusion
  (1 shorter events, 0.0 us)
Async XLA Ops:
  6.5 101.4 %all-gather.2.cloned.1.call-start = ((), (), s32[]{:S(2)}) async-start(), calls=%async_computation.1 | async-start | bytes 6684672 | tf_op jit(solution)/shard_map/all_gather | solution.py:16
  45.2 251.9 %reduce-scatter.2.cloned.1.call-start = ((), (), s32[]{:S(2)}) async-start(), calls=%async_computation.2 | async-start | bytes 13369344 | tf_op jit(solution)/shard_map/reduce_scatter | solution.py:20
  107.9 19.6 %copy-start = (bf16[384,8192]{1,0:T(8,128)(2,1)S(1)}, bf16[384,8192]{1,0:T(8,128)(2,1)}, u32[]{:S(2)}) copy-start(bf16[384,8192]{1,0:T(8,128)(2,1)} %all-gather.2.cloned.1.call-done) | copy-start | bytes 18874372
Sparse Core Ops, SparseCore 0:
  45.4 62.5 all-gather.1
  164.1 132.9 reduce-scatter.1
where the time goes:
time: 306 us
  waiting for transfers between devices  196 us (64%)
  matrix products  56.1 us (18%)
  blocking collectives  34.9 us (11%)
  between operations  13.4 us (4%)
  other arithmetic  5.67 us (2%)
    reduce_scatter x1, waiting for transfers between devices, per_device(): lax.psum_scatter(lax.dot_general(down_weight, hidden, (((0,), (1,)), ((),...  133 us
    all_gather x1, waiting for transfers between devices, per_device(): shard_rows = lax.all_gather(normed, 'row', axis=1, tiled=True)  62.6 us
    psum x1, blocking collectives, per_device(): square_sums = lax.psum(jnp.sum(float_rows * float_rows, axis=1), 'row')  34.9 us
    dot_general x1, matrix products, per_device(): lax.dot_general(down_weight, hidden, (((0,), (1,)), ((), ())), preferred_...  19.8 us
    dot_general x1, matrix products, per_device(): jnp.dot(shard_rows, gate_weight, preferred_element_type=jnp.float32)  19.6 us
    dot_general x1, matrix products, per_device(): up_proj = jnp.dot(shard_rows, up_weight, preferred_element_type=jnp.float32)  16.7 us
  transfers between devices with their start and end apart: 2, of which 2 were waited for; matrix products, arithmetic and copies ran while one was open for 0% of the time, Pallas kernels for 0%

commit v1 on v0

--- a/solution.py
+++ b/solution.py
@@ -8,7 +8,7 @@
 
 def per_device(activations, norm_gain, gate_weight, up_weight, down_weight):
     float_rows = activations.astype(jnp.float32)
-    square_sums = lax.psum(jnp.sum(float_rows * float_rows, axis=1), "row")
+    square_sums = jnp.sum(lax.all_gather(jnp.sum(float_rows * float_rows, axis=1), "row"), axis=0)
     inv_scale = lax.rsqrt(square_sums / D + 1e-05)
     normed = (float_rows * inv_scale[:, None] * norm_gain.astype(jnp.float32)[None, :]).astype(
         jnp.bfloat16

time: 306 us -> 295 us (0.964)
  blocking collectives: 34.9 us -> 23.2 us
    psum x1 -> x0, blocking collectives: 34.9 us -> none  [per_device(): square_sums = lax.psum(jnp.sum(float_rows * float_rows, axis=1), 'row')]
    all_gather x0 -> x1, blocking collectives: none -> 23.2 us  [per_device(): lax.all_gather(jnp.sum(float_rows * float_rows, axis=1), 'row')]
where the time goes in v1:
time: 295 us; the launch traced here: 294 us
  waiting for transfers between devices  196 us (66%)
  matrix products  56.1 us (19%)
  blocking collectives  23.2 us (8%)
  between operations  13.4 us (5%)
  other arithmetic  5.71 us (2%)
    reduce_scatter x1, waiting for transfers between devices, per_device(): lax.psum_scatter(lax.dot_general(down_weight, hidden, (((0,), (1,)), ((),...  133 us
    all_gather x1, waiting for transfers between devices, per_device(): shard_rows = lax.all_gather(normed, 'row', axis=1, tiled=True)  62.6 us
    all_gather x1, blocking collectives, per_device(): lax.all_gather(jnp.sum(float_rows * float_rows, axis=1), 'row')  23.2 us
    dot_general x1, matrix products, per_device(): lax.dot_general(down_weight, hidden, (((0,), (1,)), ((), ())), preferred_...  19.8 us
    dot_general x1, matrix products, per_device(): jnp.dot(shard_rows, gate_weight, preferred_element_type=jnp.float32)  19.5 us
    dot_general x1, matrix products, per_device(): up_proj = jnp.dot(shard_rows, up_weight, preferred_element_type=jnp.float32)  16.7 us
  transfers between devices with their start and end apart: 2, of which 2 were waited for; matrix products, arithmetic and copies ran while one was open for 0% of the time, Pallas kernels for 0%

profile of v1, /device:TPU:0, one launch (start us, length us, event | category | flops | bytes accessed | tf_op | source)
XLA Modules:
  0.0 294.2 jit_solution(5311400101785194598)
XLA Ops:
  6.5 0.0 all-gather.4.cloned.1.call-start
  6.5 0.7 convert_element_type.19
  7.2 1.2 fusion.1
  8.4 23.2 %all-gather.1 = f32[16,1,384]{2,1,0:T(1,128)S(1)} all-gather(f32[1,1,384]{2,1,0:T(1,128)S(1)} %reshape.7), channel_id=2, replica_groups=mesh['groups'=2,'row'=16] {'row'}, dimensions={0}, use_global_device_ids=true | all-gather | bytes 26112 | tf_op jit(solution)/shard_map/all_gather | solution.py:11
  31.6 1.9 fusion.3
  33.5 0.0 all-gather.4.cloned.1.call-update
  33.5 0.0 reduce-scatter.2.cloned.1.call-start
  33.6 62.6 %all-gather.4.cloned.1.call-done = bf16[384,8192]{1,0:T(8,128)(2,1)} async-done(((bf16[384,512]{1,0:T(8,128)(2,1)}), bf16[384,8192]{1,0:T(8,128)(2,1)}) %all-gather.4.cloned.1.call-update) | async-done | bytes 6291472 | tf_op jit(solution)/shard_map/all_gather | solution.py:16
  96.2 0.0 copy-start
  96.2 19.5 %fusion.4 = f32[384,1792]{1,0:T(8,128)} fusion(bf16[384,8192]{1,0:T(8,128)(2,1)} %all-gather.4.cloned.1.call-done, bf16[8192,1792]{1,0:T(8,128)(2,1)} %param.7), kind=kOutput, calls=%fused_computation.10 | convolution fusion | flops 11274289152 | bytes 38404096 | tf_op jit(solution)/shard_map/dot_general | solution.py:17
  115.8 0.0 copy-done
  115.8 16.7 %fusion = bf16[384,1792]{1,0:T(8,128)(2,1)S(1)} fusion(bf16[384,8192]{1,0:T(8,128)(2,1)S(1)} %copy-done, bf16[8192,1792]{1,0:T(8,128)(2,1)} %param.8, f32[384,1792]{1,0:T(8,128)} %fusion.4), kind=kOutput, calls=%fused_computation.2 | convolution fusion | flops 11278417920 | bytes 39780352 | tf_op jit(solution)/shard_map/dot_general | solution.py:18
  132.5 19.8 %convolution_bitcast_fusion = f32[8192,384]{0,1:T(8,128)} fusion(bf16[384,1792]{1,0:T(8,128)(2,1)S(1)} %fusion, bf16[1792,8192]{1,0:T(8,128)(2,1)} %param.9), kind=kOutput, calls=%fused_computation | convolution fusion | flops 11274289152 | bytes 43319296 | tf_op jit(solution)/shard_map/dot_general | solution.py:21
  152.3 0.0 reduce-scatter.2.cloned.1.call-update
  152.3 133.1 %reduce-scatter.2.cloned.1.call-done = f32[512,384]{0,1:T(8,128)} async-done(((f32[8192,384]{0,1:T(8,128)}), f32[512,384]{0,1:T(8,128)}) %reduce-scatter.2.cloned.1.call-update) | async-done | bytes 786448 | tf_op jit(solution)/shard_map/reduce_scatter | solution.py:20
  285.4 1.9 convert_bitcast_fusion
  (3 shorter events, 0.1 us)
Async XLA Ops:
  6.5 89.7 %all-gather.4.cloned.1.call-start = ((), (), s32[]{:S(2)}) async-start(), calls=%async_computation.1 | async-start | bytes 6684672 | tf_op jit(solution)/shard_map/all_gather | solution.py:16
  33.5 251.9 %reduce-scatter.2.cloned.1.call-start = ((), (), s32[]{:S(2)}) async-start(), calls=%async_computation.2 | async-start | bytes 13369344 | tf_op jit(solution)/shard_map/reduce_scatter | solution.py:20
  96.2 19.6 %copy-start = (bf16[384,8192]{1,0:T(8,128)(2,1)S(1)}, bf16[384,8192]{1,0:T(8,128)(2,1)}, u32[]{:S(2)}) copy-start(bf16[384,8192]{1,0:T(8,128)(2,1)} %all-gather.4.cloned.1.call-done) | copy-start | bytes 18874372
Sparse Core Ops, SparseCore 0:
  33.6 62.5 all-gather.3
  152.4 132.9 reduce-scatter.1
